TPU v7x, 512 devices: a whole 4x8x8 slice. The times are simulated.
512 devices in a mesh: section: 16 (over z, core), mp: 32 (over y, x).
Axes of the slice: x: 4, y: 8, z: 8, core: 2. Of those that a mesh axis runs over, the one named last changes fastest.
Arguments:
- hidden_in: bfloat16 [16, 384, 8192], P('section', None, 'mp'), may hold values from -6 to 6
- positions: int32 [16, 384], replicated, may hold values from 0 to 383, as said below
- routed_rows: int32 [8, 16, 48], replicated, may hold values from 0 to 383, as said below
- gain: bfloat16 [16, 8192], P('section'), may hold values from 0.25 to 1.75
- router: bfloat16 [16, 8192], P('section'), may hold values from -0.0625 to 0.0625
- w_query: bfloat16 [16, 8192, 4096], P('section', None, 'mp')
- w_key: bfloat16 [16, 8192, 512], P('section', None, 'mp')
- w_value: bfloat16 [16, 8192, 512], P('section', None, 'mp'), may hold values from -0.0625 to 0.0625
- w_out: bfloat16 [16, 4096, 8192], P('section', None, 'mp'), may hold values from -0.09375 to 0.09375
Outputs:
- hidden_out: bfloat16 [16, 384, 8192], P('section', None, 'mp')
Inputs may be any that keep to these rules, and one draw needn't show every extreme that they name: Each micro-batch is a pack of documents; a token's position counts from its document's first token, so positions restart at 0 at every document start and rise by one otherwise; in every draw one micro-batch is a single document. `routed_rows`: each of the 8 x 16 lists holds 48 distinct token rows of its micro-batch in ascending order.
All inputs are finite; a program needn't handle non-finite values.
Results may differ from a plain program's by a relative error of at most 0.008.
Values may be sent and summed in bfloat16 or wider, within the bound.
A program may use at most 64 MiB of HBM per device.

v0:
```python
import math

import jax
import jax.numpy as jnp
from jax import lax
from jax.sharding import PartitionSpec as P

KV_HEADS = 4
HEAD_DIM = 128
TICKS = 8
GROUP = 8
ROUTED = 48


rope_base = 500000.0
norm_epsilon = 1e-05


def from_behind(shard, axis, by):
    count = lax.axis_size(axis)
    return lax.ppermute(shard, axis, [(i, (i + by) % count) for i in range(count)])


def turn_pairs(matrix, row_positions, pair_index):
    row_count, col_count = matrix.shape
    paired = matrix.reshape(row_count, col_count // 2, 2)
    frequency = jnp.exp(pair_index.astype(jnp.float32) * (-2.0 * math.log(rope_base) / HEAD_DIM))
    angles = row_positions.astype(jnp.float32)[:, None] * frequency[None, :]
    cosine = jnp.cos(angles)
    sine_value = jnp.sin(angles)
    real_part = paired[:, :, 0]
    imag_part = paired[:, :, 1]
    turned = jnp.stack(
        [real_part * cosine - imag_part * sine_value, real_part * sine_value + imag_part * cosine],
        axis=2,
    )
    return turned.reshape(row_count, col_count)


def rotate(matrix, row_positions, offset):
    col_count = matrix.shape[1]
    pair_index = (jnp.arange(col_count // 2, dtype=jnp.int32) * 2 + offset) % HEAD_DIM // 2
    return turn_pairs(matrix, row_positions, pair_index)


def rotate_mixed(matrix, row_positions, offset):
    col_count = matrix.shape[1]
    pair_index = (jnp.arange(col_count // 2, dtype=jnp.int32) * 2 + offset) // (2 * KV_HEADS)
    return turn_pairs(matrix, row_positions, pair_index)


def to_heads(block):
    row_count = block.shape[0]
    split = block.reshape(row_count, HEAD_DIM // 2, KV_HEADS, 2)
    return jnp.transpose(split, (0, 2, 1, 3)).reshape(row_count, KV_HEADS, HEAD_DIM)


def visible(token_rows, row_positions):
    causal = token_rows[:, None] >= token_rows[None, :]
    within = token_rows[:, None] - token_rows[None, :] <= row_positions[:, None]
    return causal & within


def attend(query_heads, key_heads, value_heads, allowed):
    scores = jnp.einsum(
        "qhd,khd->hqk", query_heads, key_heads, preferred_element_type=jnp.float32
    ) / math.sqrt(HEAD_DIM)
    scores = jnp.where(allowed[None, :, :], scores, -1e30)
    maximum = jnp.max(scores, axis=2, keepdims=True)
    exponent = jnp.exp(scores - maximum)
    weights = (exponent / jnp.sum(exponent, axis=2, keepdims=True)).astype(jnp.bfloat16)
    attended = jnp.einsum("hqk,khd->qhd", weights, value_heads, preferred_element_type=jnp.float32)
    return attended.astype(jnp.bfloat16).reshape(query_heads.shape[0], -1)


def on_device(hidden_in, positions, routed_rows, gain, router, w_query, w_key, w_value, w_out):
    section_count = lax.axis_size("section")
    section_index = lax.axis_index("section")
    model_index = lax.axis_index("mp")
    hidden = hidden_in[0]
    gain_row = gain[0]
    router_row = router[0]
    query_weight = w_query[0]
    key_weight = w_key[0]
    value_weight = w_value[0]
    out_weight = w_out[0]
    head_count = query_weight.shape[1] // HEAD_DIM
    key_width = key_weight.shape[1]
    global_heads = model_index * head_count + jnp.arange(head_count, dtype=jnp.int32)
    groups = global_heads // GROUP
    for step_number in range(TICKS):
        source = (section_index - step_number) % section_count
        doc_positions = lax.dynamic_index_in_dim(positions, source, 0, keepdims=False)
        token_rows = lax.dynamic_index_in_dim(
            routed_rows[step_number], section_index, 0, keepdims=False
        )
        picked = hidden[token_rows]
        widened = picked.astype(jnp.float32)
        full_rows = lax.all_gather(picked, "mp", axis=1, tiled=True)
        full_wide = full_rows.astype(jnp.float32)
        inverse_rms = lax.rsqrt(
            jnp.mean(full_wide * full_wide, axis=1, keepdims=True) + norm_epsilon
        )
        normed = (full_wide * inverse_rms * gain_row.astype(jnp.float32)[None, :]).astype(
            jnp.bfloat16
        )
        gate = jax.nn.sigmoid(jnp.dot(full_rows, router_row, preferred_element_type=jnp.float32))
        row_positions = doc_positions[token_rows]
        key_local = rotate_mixed(
            jnp.dot(normed, key_weight, preferred_element_type=jnp.float32),
            row_positions,
            model_index * key_width,
        ).astype(jnp.bfloat16)
        value_local = jnp.dot(normed, value_weight, preferred_element_type=jnp.float32).astype(
            jnp.bfloat16
        )
        key_block = lax.all_gather(key_local, "mp", axis=1, tiled=True)
        value_block = lax.all_gather(value_local, "mp", axis=1, tiled=True)
        queries = rotate(
            jnp.dot(normed, query_weight, preferred_element_type=jnp.float32),
            row_positions,
            model_index * head_count * HEAD_DIM,
        ).astype(jnp.bfloat16)
        allowed = visible(token_rows, row_positions)
        query_heads = queries.reshape(ROUTED, head_count, HEAD_DIM)
        key_heads = jnp.take(to_heads(key_block), groups, axis=1)
        value_heads = jnp.take(to_heads(value_block), groups, axis=1)
        attended = attend(query_heads, key_heads, value_heads, allowed)
        update = jnp.dot(
            lax.all_gather(attended, "mp", axis=1, tiled=True),
            out_weight,
            preferred_element_type=jnp.float32,
        )
        new_rows = (widened + gate[:, None] * update).astype(jnp.bfloat16)
        hidden = hidden.at[token_rows].set(new_rows)
        hidden = from_behind(hidden, "section", 1)
    return hidden[None, :, :]


def solution(mesh):
    placed = (
        P("section", None, "mp"),
        P(),
        P(),
        P("section", None),
        P("section", None),
        P("section", None, "mp"),
        P("section", None, "mp"),
        P("section", None, "mp"),
        P("section", None, "mp"),
    )
    return jax.shard_map(
        on_device, mesh=mesh, in_specs=placed, out_specs=P("section", None, "mp"), check_vma=False
    )
```

profile of v0, /device:TPU:1, one launch (start us, length us, event | category | flops | bytes accessed | tf_op | source)
XLA Modules:
  0.0 1417.0 jit_solution(1483328936472391677)
XLA Ops:
  3.8 33.9 %all-gather = bf16[48,8192]{1,0:T(8,128)(2,1)S(1)} all-gather(bf16[48,256]{1,0:T(8,128)(2,1)S(1)} %gather_fusion), channel_id=2, replica_groups=mesh['section'=16,'mp'=32] {'mp'}, dimensions={1}, use_global_device_ids=true | all-gather | bytes 811008 | tf_op jit(solution)/shard_map/all_gather | solution.py:99
  38.4 29.7 %all_gather.97 = bf16[48,512]{0,1:T(8,128)(2,1)S(1)} all-gather(bf16[48,16]{0,1:T(8,128)(2,1)S(1)} %convolution_convert_fusion.15), channel_id=1, replica_groups=mesh['section'=16,'mp'=32] {'mp'}, dimensions={1}, use_global_device_ids=true | all-gather | bytes 50688 | tf_op jit(solution)/shard_map/all_gather | solution.py:118
  68.2 4.1 copy.28
  72.3 4.4 dot_general.179
  76.7 4.7 fusion.148
  87.5 28.5 %all_gather.98 = bf16[48,512]{0,1:T(8,128)(2,1)S(1)} all-gather(bf16[48,16]{0,1:T(8,128)(2,1)S(1)} %bitcast.582), channel_id=1, replica_groups=mesh['section'=16,'mp'=32] {'mp'}, dimensions={1}, use_global_device_ids=true | all-gather | bytes 50688 | tf_op jit(solution)/shard_map/all_gather | solution.py:117
  117.3 36.2 %all-gather.1 = bf16[48,1,4096]{2,0,1:T(8,128)(2,1)S(1)} all-gather(bf16[48,1,128]{2,0,1:T(8,128)(2,1)S(1)} %fusion.78), channel_id=3, replica_groups=mesh['section'=16,'mp'=32] {'mp'}, dimensions={2}, use_global_device_ids=true | all-gather | bytes 405504 | tf_op jit(solution)/shard_map/all_gather | solution.py:130
  155.2 38.8 %collective-permute-start = (bf16[384,256]{1,0:T(8,128)(2,1)S(1)}, bf16[384,256]{1,0:T(8,128)(2,1)S(1)}, u32[]{:S(2)}, u32[]{:S(2)}) collective-permute-start(bf16[384,256]{1,0:T(8,128)(2,1)S(1)} %scatter_fusion), channel_id=1, source_target_pairs={{0,32},{32,64},{64,96},{96,128},{128,160},{160,192},{192,224},{224... | collective-permute-start | bytes 589832 | tf_op jit(solution)/shard_map/ppermute | solution.py:21
  201.5 31.5 %all-gather.2 = bf16[48,8192]{1,0:T(8,128)(2,1)S(1)} all-gather(bf16[48,256]{1,0:T(8,128)(2,1)S(1)} %gather_fusion.2), channel_id=4, replica_groups=mesh['section'=16,'mp'=32] {'mp'}, dimensions={1}, use_global_device_ids=true | all-gather | bytes 811008 | tf_op jit(solution)/shard_map/all_gather | solution.py:99
  237.3 29.2 %all_gather.101 = bf16[48,512]{0,1:T(8,128)(2,1)S(1)} all-gather(bf16[48,16]{0,1:T(8,128)(2,1)S(1)} %convolution_convert_fusion.14), channel_id=1, replica_groups=mesh['section'=16,'mp'=32] {'mp'}, dimensions={1}, use_global_device_ids=true | all-gather | bytes 50688 | tf_op jit(solution)/shard_map/all_gather | solution.py:118
  267.0 28.9 %all_gather.102 = bf16[48,512]{0,1:T(8,128)(2,1)S(1)} all-gather(bf16[48,16]{0,1:T(8,128)(2,1)S(1)} %bitcast.583), channel_id=1, replica_groups=mesh['section'=16,'mp'=32] {'mp'}, dimensions={1}, use_global_device_ids=true | all-gather | bytes 50688 | tf_op jit(solution)/shard_map/all_gather | solution.py:117
  296.4 36.2 %all-gather.3 = bf16[48,1,4096]{2,0,1:T(8,128)(2,1)S(1)} all-gather(bf16[48,1,128]{2,0,1:T(8,128)(2,1)S(1)} %fusion.79), channel_id=5, replica_groups=mesh['section'=16,'mp'=32] {'mp'}, dimensions={2}, use_global_device_ids=true | all-gather | bytes 405504 | tf_op jit(solution)/shard_map/all_gather | solution.py:130
  334.0 34.9 %collective-permute-start.1 = (bf16[384,256]{1,0:T(8,128)(2,1)S(1)}, bf16[384,256]{1,0:T(8,128)(2,1)S(1)}, u32[]{:S(2)}, u32[]{:S(2)}) collective-permute-start(bf16[384,256]{1,0:T(8,128)(2,1)S(1)} %scatter_custom_fusion.1), channel_id=1, source_target_pairs={{0,32},{32,64},{64,96},{96,128},{128,160},{160,192},{192,224},{224... | collective-permute-start | bytes 589832 | tf_op jit(solution)/shard_map/ppermute | solution.py:21
  372.2 30.3 %all-gather.4 = bf16[48,8192]{1,0:T(8,128)(2,1)S(1)} all-gather(bf16[48,256]{1,0:T(8,128)(2,1)S(1)} %gather_fusion.4), channel_id=6, replica_groups=mesh['section'=16,'mp'=32] {'mp'}, dimensions={1}, use_global_device_ids=true | all-gather | bytes 811008 | tf_op jit(solution)/shard_map/all_gather | solution.py:99
  406.5 29.1 %all_gather.105 = bf16[48,512]{0,1:T(8,128)(2,1)S(1)} all-gather(bf16[48,16]{0,1:T(8,128)(2,1)S(1)} %convolution_convert_fusion.13), channel_id=1, replica_groups=mesh['section'=16,'mp'=32] {'mp'}, dimensions={1}, use_global_device_ids=true | all-gather | bytes 50688 | tf_op jit(solution)/shard_map/all_gather | solution.py:118
  436.1 29.3 %all_gather.106 = bf16[48,512]{0,1:T(8,128)(2,1)S(1)} all-gather(bf16[48,16]{0,1:T(8,128)(2,1)S(1)} %bitcast.584), channel_id=1, replica_groups=mesh['section'=16,'mp'=32] {'mp'}, dimensions={1}, use_global_device_ids=true | all-gather | bytes 50688 | tf_op jit(solution)/shard_map/all_gather | solution.py:117
  465.9 36.4 %all-gather.5 = bf16[48,1,4096]{2,0,1:T(8,128)(2,1)S(1)} all-gather(bf16[48,1,128]{2,0,1:T(8,128)(2,1)S(1)} %fusion.80), channel_id=7, replica_groups=mesh['section'=16,'mp'=32] {'mp'}, dimensions={2}, use_global_device_ids=true | all-gather | bytes 405504 | tf_op jit(solution)/shard_map/all_gather | solution.py:130
  503.7 38.5 %collective-permute-start.2 = (bf16[384,256]{1,0:T(8,128)(2,1)S(1)}, bf16[384,256]{1,0:T(8,128)(2,1)S(1)}, u32[]{:S(2)}, u32[]{:S(2)}) collective-permute-start(bf16[384,256]{1,0:T(8,128)(2,1)S(1)} %scatter_custom_fusion.2), channel_id=1, source_target_pairs={{0,32},{32,64},{64,96},{96,128},{128,160},{160,192},{192,224},{224... | collective-permute-start | bytes 589832 | tf_op jit(solution)/shard_map/ppermute | solution.py:21
  545.9 30.5 %all-gather.6 = bf16[48,8192]{1,0:T(8,128)(2,1)S(1)} all-gather(bf16[48,256]{1,0:T(8,128)(2,1)S(1)} %gather_fusion.6), channel_id=8, replica_groups=mesh['section'=16,'mp'=32] {'mp'}, dimensions={1}, use_global_device_ids=true | all-gather | bytes 811008 | tf_op jit(solution)/shard_map/all_gather | solution.py:99
  580.3 28.7 %all_gather.109 = bf16[48,512]{0,1:T(8,128)(2,1)S(1)} all-gather(bf16[48,16]{0,1:T(8,128)(2,1)S(1)} %convolution_convert_fusion.12), channel_id=1, replica_groups=mesh['section'=16,'mp'=32] {'mp'}, dimensions={1}, use_global_device_ids=true | all-gather | bytes 50688 | tf_op jit(solution)/shard_map/all_gather | solution.py:118
  609.5 29.0 %all_gather.110 = bf16[48,512]{0,1:T(8,128)(2,1)S(1)} all-gather(bf16[48,16]{0,1:T(8,128)(2,1)S(1)} %bitcast.585), channel_id=1, replica_groups=mesh['section'=16,'mp'=32] {'mp'}, dimensions={1}, use_global_device_ids=true | all-gather | bytes 50688 | tf_op jit(solution)/shard_map/all_gather | solution.py:117
  639.1 36.4 %all-gather.7 = bf16[48,1,4096]{2,0,1:T(8,128)(2,1)S(1)} all-gather(bf16[48,1,128]{2,0,1:T(8,128)(2,1)S(1)} %fusion.81), channel_id=9, replica_groups=mesh['section'=16,'mp'=32] {'mp'}, dimensions={2}, use_global_device_ids=true | all-gather | bytes 405504 | tf_op jit(solution)/shard_map/all_gather | solution.py:130
  676.9 38.5 %collective-permute-start.3 = (bf16[384,256]{1,0:T(8,128)(2,1)S(1)}, bf16[384,256]{1,0:T(8,128)(2,1)S(1)}, u32[]{:S(2)}, u32[]{:S(2)}) collective-permute-start(bf16[384,256]{1,0:T(8,128)(2,1)S(1)} %scatter_custom_fusion.3), channel_id=1, source_target_pairs={{0,32},{32,64},{64,96},{96,128},{128,160},{160,192},{192,224},{224... | collective-permute-start | bytes 589832 | tf_op jit(solution)/shard_map/ppermute | solution.py:21
  716.7 2.5 collective-permute-done.3
  719.9 30.7 %all-gather.8 = bf16[48,8192]{1,0:T(8,128)(2,1)S(1)} all-gather(bf16[48,256]{1,0:T(8,128)(2,1)S(1)} %gather_fusion.8), channel_id=10, replica_groups=mesh['section'=16,'mp'=32] {'mp'}, dimensions={1}, use_global_device_ids=true | all-gather | bytes 811008 | tf_op jit(solution)/shard_map/all_gather | solution.py:99
  754.5 28.7 %all_gather.113 = bf16[48,512]{0,1:T(8,128)(2,1)S(1)} all-gather(bf16[48,16]{0,1:T(8,128)(2,1)S(1)} %convolution_convert_fusion.11), channel_id=1, replica_groups=mesh['section'=16,'mp'=32] {'mp'}, dimensions={1}, use_global_device_ids=true | all-gather | bytes 50688 | tf_op jit(solution)/shard_map/all_gather | solution.py:118
  783.7 29.0 %all_gather.114 = bf16[48,512]{0,1:T(8,128)(2,1)S(1)} all-gather(bf16[48,16]{0,1:T(8,128)(2,1)S(1)} %bitcast.586), channel_id=1, replica_groups=mesh['section'=16,'mp'=32] {'mp'}, dimensions={1}, use_global_device_ids=true | all-gather | bytes 50688 | tf_op jit(solution)/shard_map/all_gather | solution.py:117
  813.2 36.4 %all-gather.9 = bf16[48,1,4096]{2,0,1:T(8,128)(2,1)S(1)} all-gather(bf16[48,1,128]{2,0,1:T(8,128)(2,1)S(1)} %fusion.82), channel_id=11, replica_groups=mesh['section'=16,'mp'=32] {'mp'}, dimensions={2}, use_global_device_ids=true | all-gather | bytes 405504 | tf_op jit(solution)/shard_map/all_gather | solution.py:130
  851.0 37.5 %collective-permute-start.4 = (bf16[384,256]{1,0:T(8,128)(2,1)S(1)}, bf16[384,256]{1,0:T(8,128)(2,1)S(1)}, u32[]{:S(2)}, u32[]{:S(2)}) collective-permute-start(bf16[384,256]{1,0:T(8,128)(2,1)S(1)} %scatter_custom_fusion.4), channel_id=1, source_target_pairs={{0,32},{32,64},{64,96},{96,128},{128,160},{160,192},{192,224},{224... | collective-permute-start | bytes 589832 | tf_op jit(solution)/shard_map/ppermute | solution.py:21
  890.1 3.4 collective-permute-done.4
  894.1 30.5 %all-gather.10 = bf16[48,8192]{1,0:T(8,128)(2,1)S(1)} all-gather(bf16[48,256]{1,0:T(8,128)(2,1)S(1)} %gather_fusion.10), channel_id=12, replica_groups=mesh['section'=16,'mp'=32] {'mp'}, dimensions={1}, use_global_device_ids=true | all-gather | bytes 811008 | tf_op jit(solution)/shard_map/all_gather | solution.py:99
  928.5 28.7 %all_gather.117 = bf16[48,512]{0,1:T(8,128)(2,1)S(1)} all-gather(bf16[48,16]{0,1:T(8,128)(2,1)S(1)} %convolution_convert_fusion.10), channel_id=1, replica_groups=mesh['section'=16,'mp'=32] {'mp'}, dimensions={1}, use_global_device_ids=true | all-gather | bytes 50688 | tf_op jit(solution)/shard_map/all_gather | solution.py:118
  957.7 29.1 %all_gather.118 = bf16[48,512]{0,1:T(8,128)(2,1)S(1)} all-gather(bf16[48,16]{0,1:T(8,128)(2,1)S(1)} %bitcast.587), channel_id=1, replica_groups=mesh['section'=16,'mp'=32] {'mp'}, dimensions={1}, use_global_device_ids=true | all-gather | bytes 50688 | tf_op jit(solution)/shard_map/all_gather | solution.py:117
  987.3 36.5 %all-gather.11 = bf16[48,1,4096]{2,0,1:T(8,128)(2,1)S(1)} all-gather(bf16[48,1,128]{2,0,1:T(8,128)(2,1)S(1)} %fusion.83), channel_id=13, replica_groups=mesh['section'=16,'mp'=32] {'mp'}, dimensions={2}, use_global_device_ids=true | all-gather | bytes 405504 | tf_op jit(solution)/shard_map/all_gather | solution.py:130
  1025.2 36.5 %collective-permute-start.5 = (bf16[384,256]{1,0:T(8,128)(2,1)S(1)}, bf16[384,256]{1,0:T(8,128)(2,1)S(1)}, u32[]{:S(2)}, u32[]{:S(2)}) collective-permute-start(bf16[384,256]{1,0:T(8,128)(2,1)S(1)} %scatter_custom_fusion.5), channel_id=1, source_target_pairs={{0,32},{32,64},{64,96},{96,128},{128,160},{160,192},{192,224},{224... | collective-permute-start | bytes 589832 | tf_op jit(solution)/shard_map/ppermute | solution.py:21
  1063.1 4.5 collective-permute-done.5
  1068.3 30.5 %all-gather.12 = bf16[48,8192]{1,0:T(8,128)(2,1)S(1)} all-gather(bf16[48,256]{1,0:T(8,128)(2,1)S(1)} %gather_fusion.12), channel_id=14, replica_groups=mesh['section'=16,'mp'=32] {'mp'}, dimensions={1}, use_global_device_ids=true | all-gather | bytes 811008 | tf_op jit(solution)/shard_map/all_gather | solution.py:99
  1102.7 28.7 %all_gather.121 = bf16[48,512]{0,1:T(8,128)(2,1)S(1)} all-gather(bf16[48,16]{0,1:T(8,128)(2,1)S(1)} %convolution_convert_fusion.9), channel_id=1, replica_groups=mesh['section'=16,'mp'=32] {'mp'}, dimensions={1}, use_global_device_ids=true | all-gather | bytes 50688 | tf_op jit(solution)/shard_map/all_gather | solution.py:118
  1131.9 29.0 %all_gather.122 = bf16[48,512]{0,1:T(8,128)(2,1)S(1)} all-gather(bf16[48,16]{0,1:T(8,128)(2,1)S(1)} %bitcast.588), channel_id=1, replica_groups=mesh['section'=16,'mp'=32] {'mp'}, dimensions={1}, use_global_device_ids=true | all-gather | bytes 50688 | tf_op jit(solution)/shard_map/all_gather | solution.py:117
  1161.5 36.4 %all-gather.13 = bf16[48,1,4096]{2,0,1:T(8,128)(2,1)S(1)} all-gather(bf16[48,1,128]{2,0,1:T(8,128)(2,1)S(1)} %fusion.84), channel_id=15, replica_groups=mesh['section'=16,'mp'=32] {'mp'}, dimensions={2}, use_global_device_ids=true | all-gather | bytes 405504 | tf_op jit(solution)/shard_map/all_gather | solution.py:130
  1199.2 35.4 %collective-permute-start.6 = (bf16[384,256]{1,0:T(8,128)(2,1)S(1)}, bf16[384,256]{1,0:T(8,128)(2,1)S(1)}, u32[]{:S(2)}, u32[]{:S(2)}) collective-permute-start(bf16[384,256]{1,0:T(8,128)(2,1)S(1)} %scatter_custom_fusion.6), channel_id=1, source_target_pairs={{0,32},{32,64},{64,96},{96,128},{128,160},{160,192},{192,224},{224... | collective-permute-start | bytes 589832 | tf_op jit(solution)/shard_map/ppermute | solution.py:21
  1236.1 5.5 collective-permute-done.6
  1242.3 30.7 %all-gather.14 = bf16[48,8192]{1,0:T(8,128)(2,1)S(1)} all-gather(bf16[48,256]{1,0:T(8,128)(2,1)S(1)} %gather_fusion.14), channel_id=16, replica_groups=mesh['section'=16,'mp'=32] {'mp'}, dimensions={1}, use_global_device_ids=true | all-gather | bytes 811008 | tf_op jit(solution)/shard_map/all_gather | solution.py:99
  1277.0 28.7 %all_gather.125 = bf16[48,512]{0,1:T(8,128)(2,1)S(1)} all-gather(bf16[48,16]{0,1:T(8,128)(2,1)S(1)} %convolution_convert_fusion.8), channel_id=1, replica_groups=mesh['section'=16,'mp'=32] {'mp'}, dimensions={1}, use_global_device_ids=true | all-gather | bytes 50688 | tf_op jit(solution)/shard_map/all_gather | solution.py:118
  1306.2 29.0 %all_gather.126 = bf16[48,512]{0,1:T(8,128)(2,1)S(1)} all-gather(bf16[48,16]{0,1:T(8,128)(2,1)S(1)} %bitcast.589), channel_id=1, replica_groups=mesh['section'=16,'mp'=32] {'mp'}, dimensions={1}, use_global_device_ids=true | all-gather | bytes 50688 | tf_op jit(solution)/shard_map/all_gather | solution.py:117
  1335.7 36.4 %all-gather.15 = bf16[48,1,4096]{2,0,1:T(8,128)(2,1)S(1)} all-gather(bf16[48,1,128]{2,0,1:T(8,128)(2,1)S(1)} %fusion.85), channel_id=17, replica_groups=mesh['section'=16,'mp'=32] {'mp'}, dimensions={2}, use_global_device_ids=true | all-gather | bytes 405504 | tf_op jit(solution)/shard_map/all_gather | solution.py:130
  1373.5 34.3 %collective-permute-start.7 = (bf16[384,256]{1,0:T(8,128)(2,1)S(1)}, bf16[384,256]{1,0:T(8,128)(2,1)S(1)}, u32[]{:S(2)}, u32[]{:S(2)}) collective-permute-start(bf16[384,256]{1,0:T(8,128)(2,1)S(1)} %scatter_custom_fusion.7), channel_id=1, source_target_pairs={{0,32},{32,64},{64,96},{96,128},{128,160},{160,192},{192,224},{224... | collective-permute-start | bytes 589832 | tf_op jit(solution)/shard_map/ppermute | solution.py:21
  1407.8 8.1 collective-permute-done.7
  (260 shorter events, 81.4 us)
Async XLA Ops:
  0.0 153.8 %copy-start = (bf16[1,4096,256]{2,1,0:T(8,128)(2,1)S(1)}, bf16[1,4096,256]{2,1,0:T(8,128)(2,1)}, u32[]{:S(2)}) copy-start(bf16[1,4096,256]{2,1,0:T(8,128)(2,1)} %param.19) | copy-start | bytes 6291460
  0.0 37.6 %copy-start.13 = (bf16[1,8192]{1,0:T(2,128)(2,1)S(1)}, bf16[1,8192]{1,0:T(2,128)(2,1)}, u32[]{:S(2)}) copy-start(bf16[1,8192]{1,0:T(2,128)(2,1)} %param.14) | copy-start | bytes 49156
  2.5 1.2 copy-start.16
  3.8 34.2 %copy-start.20 = (bf16[1,8192,16]{1,2,0:T(8,128)(2,1)S(1)}, bf16[1,8192,16]{1,2,0:T(8,128)(2,1)}, u32[]{:S(2)}) copy-start(bf16[1,8192,16]{1,2,0:T(8,128)(2,1)} %param.18) | copy-start | bytes 786436
  37.7 34.6 %copy-start.14 = (f32[1,8192]{1,0:T(1,128)}, f32[1,8192]{1,0:T(1,128)S(1)}, u32[]{:S(2)}) copy-start(f32[1,8192]{1,0:T(1,128)S(1)} %mul.1050) | copy-start | bytes 98308
  38.0 38.7 %copy-start.24 = (f32[48]{0:T(128)}, f32[48]{0:T(128)S(1)}, u32[]{:S(2)}) copy-start(f32[48]{0:T(128)S(1)} %add_rsqrt_fusion.7) | copy-start | bytes 580
  76.7 8.3 copy-start.8
  81.5 2.8 copy-start.10
  83.3 0.9 copy-start.18
  85.0 31.1 %copy-start.19 = (s32[48]{0:T(128)S(1)}, s32[48]{0:T(128)}, u32[]{:S(2)}) copy-start(s32[48]{0:T(128)} %copy-done.18) | copy-start | bytes 580
  85.9 30.2 %copy-start.12 = (bf16[48,64,2]{0,2,1:T(2,128)(2,1)S(1)}, bf16[48,64,2]{0,2,1:T(2,128)(2,1)}, u32[]{:S(2)}) copy-start(bf16[48,64,2]{0,2,1:T(2,128)(2,1)} %copy.30) | copy-start | bytes 36868
  85.9 67.6 %copy-start.22 = (bf16[1,8192]{1,0:T(2,128)(2,1)S(1)}, bf16[1,8192]{1,0:T(2,128)(2,1)}, u32[]{:S(2)}) copy-start(bf16[1,8192]{1,0:T(2,128)(2,1)} %param.15) | copy-start | bytes 49156
  153.5 0.8 copy-start.17
  155.2 45.6 %collective-permute-start = (bf16[384,256]{1,0:T(8,128)(2,1)S(1)}, bf16[384,256]{1,0:T(8,128)(2,1)S(1)}, u32[]{:S(2)}, u32[]{:S(2)}) collective-permute-start(bf16[384,256]{1,0:T(8,128)(2,1)S(1)} %scatter_fusion), channel_id=1, source_target_pairs={{0,32},{32,64},{64,96},{96,128},{128,160},{160,192},{192,224},{224... | collective-permute-start | bytes 589832 | tf_op jit(solution)/shard_map/ppermute | solution.py:21
  197.0 36.2 %copy-start.15 = (f32[1,8192]{1,0:T(1,128)S(1)}, f32[1,8192]{1,0:T(1,128)}, u32[]{:S(2)}) copy-start(f32[1,8192]{1,0:T(1,128)} %copy-done.14) | copy-start | bytes 98308
  197.0 36.2 %copy-start.21 = (bf16[1,8192,16]{1,2,0:T(8,128)(2,1)S(1)}, bf16[1,8192,16]{1,2,0:T(8,128)(2,1)}, u32[]{:S(2)}) copy-start(bf16[1,8192,16]{1,2,0:T(8,128)(2,1)} %param.18) | copy-start | bytes 786436
  201.4 32.2 %copy-start.1 = (bf16[64,2,8192]{2,1,0:T(2,128)(2,1)S(1)}, bf16[64,2,8192]{2,1,0:T(2,128)(2,1)}, u32[]{:S(2)}) copy-start(bf16[64,2,8192]{2,1,0:T(2,128)(2,1)} %dot_general.179) | copy-start | bytes 6291460
  233.7 2.5 copy-start.9
  236.2 0.8 copy-start.23
  236.2 30.3 %copy-start.11 = (f32[64]{0:T(128)S(1)}, f32[64]{0:T(128)}, u32[]{:S(2)}) copy-start(f32[64]{0:T(128)} %copy-done.10) | copy-start | bytes 772
  334.0 37.6 %collective-permute-start.1 = (bf16[384,256]{1,0:T(8,128)(2,1)S(1)}, bf16[384,256]{1,0:T(8,128)(2,1)S(1)}, u32[]{:S(2)}, u32[]{:S(2)}) collective-permute-start(bf16[384,256]{1,0:T(8,128)(2,1)S(1)} %scatter_custom_fusion.1), channel_id=1, source_target_pairs={{0,32},{32,64},{64,96},{96,128},{128,160},{160,192},{192,224},{224... | collective-permute-start | bytes 589832 | tf_op jit(solution)/shard_map/ppermute | solution.py:21
  372.2 31.0 %copy-start.2 = (bf16[64,2,8192]{2,1,0:T(2,128)(2,1)S(1)}, bf16[64,2,8192]{2,1,0:T(2,128)(2,1)}, u32[]{:S(2)}) copy-start(bf16[64,2,8192]{2,1,0:T(2,128)(2,1)} %dot_general.179) | copy-start | bytes 6291460
  503.7 41.5 %collective-permute-start.2 = (bf16[384,256]{1,0:T(8,128)(2,1)S(1)}, bf16[384,256]{1,0:T(8,128)(2,1)S(1)}, u32[]{:S(2)}, u32[]{:S(2)}) collective-permute-start(bf16[384,256]{1,0:T(8,128)(2,1)S(1)} %scatter_custom_fusion.2), channel_id=1, source_target_pairs={{0,32},{32,64},{64,96},{96,128},{128,160},{160,192},{192,224},{224... | collective-permute-start | bytes 589832 | tf_op jit(solution)/shard_map/ppermute | solution.py:21
  545.9 31.2 %copy-start.3 = (bf16[64,2,8192]{2,1,0:T(2,128)(2,1)S(1)}, bf16[64,2,8192]{2,1,0:T(2,128)(2,1)}, u32[]{:S(2)}) copy-start(bf16[64,2,8192]{2,1,0:T(2,128)(2,1)} %dot_general.179) | copy-start | bytes 6291460
  676.9 42.4 %collective-permute-start.3 = (bf16[384,256]{1,0:T(8,128)(2,1)S(1)}, bf16[384,256]{1,0:T(8,128)(2,1)S(1)}, u32[]{:S(2)}, u32[]{:S(2)}) collective-permute-start(bf16[384,256]{1,0:T(8,128)(2,1)S(1)} %scatter_custom_fusion.3), channel_id=1, source_target_pairs={{0,32},{32,64},{64,96},{96,128},{128,160},{160,192},{192,224},{224... | collective-permute-start | bytes 589832 | tf_op jit(solution)/shard_map/ppermute | solution.py:21
  719.9 31.4 %copy-start.4 = (bf16[64,2,8192]{2,1,0:T(2,128)(2,1)S(1)}, bf16[64,2,8192]{2,1,0:T(2,128)(2,1)}, u32[]{:S(2)}) copy-start(bf16[64,2,8192]{2,1,0:T(2,128)(2,1)} %dot_general.179) | copy-start | bytes 6291460
  851.0 42.4 %collective-permute-start.4 = (bf16[384,256]{1,0:T(8,128)(2,1)S(1)}, bf16[384,256]{1,0:T(8,128)(2,1)S(1)}, u32[]{:S(2)}, u32[]{:S(2)}) collective-permute-start(bf16[384,256]{1,0:T(8,128)(2,1)S(1)} %scatter_custom_fusion.4), channel_id=1, source_target_pairs={{0,32},{32,64},{64,96},{96,128},{128,160},{160,192},{192,224},{224... | collective-permute-start | bytes 589832 | tf_op jit(solution)/shard_map/ppermute | solution.py:21
  894.1 31.2 %copy-start.5 = (bf16[64,2,8192]{2,1,0:T(2,128)(2,1)S(1)}, bf16[64,2,8192]{2,1,0:T(2,128)(2,1)}, u32[]{:S(2)}) copy-start(bf16[64,2,8192]{2,1,0:T(2,128)(2,1)} %dot_general.179) | copy-start | bytes 6291460
  1025.2 42.4 %collective-permute-start.5 = (bf16[384,256]{1,0:T(8,128)(2,1)S(1)}, bf16[384,256]{1,0:T(8,128)(2,1)S(1)}, u32[]{:S(2)}, u32[]{:S(2)}) collective-permute-start(bf16[384,256]{1,0:T(8,128)(2,1)S(1)} %scatter_custom_fusion.5), channel_id=1, source_target_pairs={{0,32},{32,64},{64,96},{96,128},{128,160},{160,192},{192,224},{224... | collective-permute-start | bytes 589832 | tf_op jit(solution)/shard_map/ppermute | solution.py:21
  1068.3 31.2 %copy-start.6 = (bf16[64,2,8192]{2,1,0:T(2,128)(2,1)S(1)}, bf16[64,2,8192]{2,1,0:T(2,128)(2,1)}, u32[]{:S(2)}) copy-start(bf16[64,2,8192]{2,1,0:T(2,128)(2,1)} %dot_general.179) | copy-start | bytes 6291460
  1199.2 42.4 %collective-permute-start.6 = (bf16[384,256]{1,0:T(8,128)(2,1)S(1)}, bf16[384,256]{1,0:T(8,128)(2,1)S(1)}, u32[]{:S(2)}, u32[]{:S(2)}) collective-permute-start(bf16[384,256]{1,0:T(8,128)(2,1)S(1)} %scatter_custom_fusion.6), channel_id=1, source_target_pairs={{0,32},{32,64},{64,96},{96,128},{128,160},{160,192},{192,224},{224... | collective-permute-start | bytes 589832 | tf_op jit(solution)/shard_map/ppermute | solution.py:21
  1242.3 31.4 %copy-start.7 = (bf16[64,2,8192]{2,1,0:T(2,128)(2,1)S(1)}, bf16[64,2,8192]{2,1,0:T(2,128)(2,1)}, u32[]{:S(2)}) copy-start(bf16[64,2,8192]{2,1,0:T(2,128)(2,1)} %dot_general.179) | copy-start | bytes 6291460
  1373.5 42.4 %collective-permute-start.7 = (bf16[384,256]{1,0:T(8,128)(2,1)S(1)}, bf16[384,256]{1,0:T(8,128)(2,1)S(1)}, u32[]{:S(2)}, u32[]{:S(2)}) collective-permute-start(bf16[384,256]{1,0:T(8,128)(2,1)S(1)} %scatter_custom_fusion.7), channel_id=1, source_target_pairs={{0,32},{32,64},{64,96},{96,128},{128,160},{160,192},{192,224},{224... | collective-permute-start | bytes 589832 | tf_op jit(solution)/shard_map/ppermute | solution.py:21
where the time goes:
time: 1430 us; the launch traced here: 1420 us
  blocking collectives  1000 us (70%)
  starting transfers between devices  295 us (21%)
  matrix products  40.1 us (3%)
  local copies, waits for them, and re-layouts  34.8 us (2%)
  waiting for transfers between devices  26.8 us (2%)
  other arithmetic  17 us (1%)
    ppermute x8, starting transfers between devices, from_behind(): lax.ppermute(shard, axis, [(i, (i + by) % count) for i in range(count)])  295 us
    all_gather x8, blocking collectives, on_device(): lax.all_gather(attended, 'mp', axis=1, tiled=True)  291 us
    all_gather x8, blocking collectives, on_device(): full_rows = lax.all_gather(picked, 'mp', axis=1, tiled=True)  249 us
    all_gather x8, blocking collectives, on_device(): key_block = lax.all_gather(key_local, 'mp', axis=1, tiled=True)  232 us
    all_gather x8, blocking collectives, on_device(): value_block = lax.all_gather(value_local, 'mp', axis=1, tiled=True)  231 us
  transfers between devices with their start and end apart: 8, of which 7 were waited for; matrix products, arithmetic and copies ran while one was open for 1% of the time, Pallas kernels for 0%

commit v1 on v0

v1 whole, which is shorter than its diff:
```python
import functools
import math

import jax
import jax.numpy as jnp
from jax import lax
from jax.experimental import pallas as pl
from jax.experimental.pallas import tpu as pltpu
from jax.sharding import PartitionSpec as P

KV_HEADS = 4
HEAD_DIM = 128
TICKS = 8
GROUP = 8
ROUTED = 48
NX = 4
NY = 8

rope_base = 500000.0
norm_epsilon = 1e-05

MESH = pl.DeviceIdType.MESH
F32 = jnp.float32
BF16 = jnp.bfloat16
ORDER = (0, 1, 7, 2, 6, 3, 5, 4)


def dot(a, b):
    return jnp.dot(a, b, preferred_element_type=F32)


def dot_nt(a, b):
    return lax.dot_general(a, b, (((1,), (1,)), ((), ())), preferred_element_type=F32)


def dot_tn(a, b):
    return lax.dot_general(a, b, (((0,), (0,)), ((), ())), preferred_element_type=F32)


def kernel(
    sections,
    hidden_ref, weight_ref, out_weight_ref, gain_ref, router_ref,
    cos_ref, sin_ref, seen_ref, rows_ref, next_rows_ref,
    o_ref,
    hid, picked, picked_out, blocks, kv_tiles, kv_all, att, att_blocks,
    hid_send, hid_recv, picked_send, picked_recv,
    ys1, yr1, xs1, xr1, rs1, rr1,
    ys3, yr3, xs3, xr3, rs3, rr3,
    kys, kyr, kxs, kxr,
):
    s = lax.axis_index("section")
    m = lax.axis_index("mp")
    x = lax.rem(m, NX)
    y = lax.div(m, NX)
    after = lax.rem(s + 1, sections)
    before = lax.rem(s + sections - 1, sections)

    def at_y(d):
        return lax.rem(y + d + NY, NY)

    def at_x(d):
        return lax.rem(x + d + NX, NX)

    def dev(yy, xx):
        return (s, yy * NX + xx)

    barrier = pltpu.get_barrier_semaphore()
    peers = [dev(at_y(d), x) for d in range(1, NY)] + [dev(y, at_x(d)) for d in range(1, NX)]
    peers += [(after, m), (before, m)]
    for peer in peers:
        pl.semaphore_signal(barrier, inc=1, device_id=peer, device_id_type=MESH)

    def remote(src, dst, send, recv, to):
        return pltpu.make_async_remote_copy(
            src_ref=src, dst_ref=dst, send_sem=send, recv_sem=recv, device_id=to, device_id_type=MESH
        )

    def gather(own, into, sems, consume):
        ys, yr, xs, xr, rs, rr = sems
        right = dev(y, at_x(1))
        left = dev(y, at_x(-1))

        def slot(j, xx):
            return at_y(-j) * NX + xx

        def y_copy(j, source_y):
            return remote(own, into.at[source_y * NX + x], ys.at[j], yr.at[j], dev(at_y(j), x))

        def x_copy(j, way, src, src_x):
            to = right if way == 0 else left
            return remote(src, into.at[slot(j, src_x)], xs.at[2 * j + way], xr.at[2 * j + way], to)

        def r_copy(j, src_x):
            to = right if j % 2 == 0 else left
            block = into.at[slot(j, src_x)]
            return remote(block, block, rs.at[j], rr.at[j], to)

        for j in (4, 3, 5, 2, 6, 1, 7):
            y_copy(j, y).start()
        sent = []
        for t in range(NY + 2):
            if t < NY:
                j = ORDER[t]
                if j == 0:
                    mine = own
                else:
                    y_copy(j, at_y(-j)).wait_recv()
                    mine = into.at[slot(j, x)]
                for way in (0, 1):
                    copy = x_copy(j, way, mine, x)
                    copy.start()
                    sent.append(copy)
                consume(mine, slot(j, x))
            if 1 <= t <= NY:
                j = ORDER[t - 1]
                for way, src_x in ((0, at_x(-1)), (1, at_x(1))):
                    x_copy(j, way, into.at[slot(j, src_x)], src_x).wait_recv()
                    if j % 2 == way:
                        copy = r_copy(j, src_x)
                        copy.start()
                        sent.append(copy)
                    consume(into.at[slot(j, src_x)], slot(j, src_x))
            if t >= 2:
                j = ORDER[t - 2]
                r_copy(j, at_x(2)).wait_recv()
                consume(into.at[slot(j, at_x(2))], slot(j, at_x(2)))

        def finish():
            for j in range(1, NY):
                y_copy(j, y).wait_send()
            for copy in sent:
                copy.wait_send()

        return finish

    hid[0] = hidden_ref[...]
    kv_tiles[...] = jnp.zeros_like(kv_tiles)
    picked[0] = dot(rows_ref[0], hidden_ref[...]).astype(BF16)

    def entry_row(d):
        source = lax.shift_right_logical(d, 2)
        sy = lax.shift_right_logical(source, 2)
        sx = lax.bitwise_and(source, 3)
        return (sx * NY + sy) * 8 + lax.bitwise_and(d, 3)

    d0 = lax.broadcasted_iota(jnp.int32, (HEAD_DIM, 256), 0)
    c1 = lax.broadcasted_iota(jnp.int32, (HEAD_DIM, 256), 1)
    key_place = (entry_row(d0) == c1).astype(F32).astype(BF16)
    r0 = lax.broadcasted_iota(jnp.int32, (256, HEAD_DIM), 0)
    d1 = lax.broadcasted_iota(jnp.int32, (256, HEAD_DIM), 1)
    value_place = (entry_row(d1) + 4 == r0).astype(F32).astype(BF16)
    t0 = lax.broadcasted_iota(jnp.int32, (32, 128), 0)
    k1 = lax.broadcasted_iota(jnp.int32, (32, 128), 1)
    head = lax.shift_right_logical(t0, 3)
    is_value = lax.bitwise_and(lax.shift_right_logical(t0, 2), 1)
    pair = lax.bitwise_and(lax.shift_right_logical(t0, 1), 1)
    tile_place = (16 * is_value + 8 * pair + 2 * head + lax.bitwise_and(t0, 1) == k1).astype(F32).astype(BF16)
    even = lax.bitwise_and(lax.broadcasted_iota(jnp.int32, (ROUTED, 256), 1), 1) == 0
    ones = jnp.ones((ROUTED, 128), BF16)

    pl.semaphore_wait(barrier, len(peers))

    def hid_copy(n):
        return remote(hid.at[n], hid.at[n + 1], hid_send.at[n], hid_recv.at[n + 1], (after, m))

    def picked_copy(n):
        return remote(picked_out.at[n], picked.at[n + 1], picked_send.at[n], picked_recv.at[n + 1], (after, m))

    def tick(n, carry):
        @pl.when(n > 0)
        def _():
            picked_copy(n - 1).wait_recv()

        state = {
            "acc": jnp.zeros((ROUTED, 256), F32),
            "squares": jnp.zeros((ROUTED, 256), F32),
            "routed": jnp.zeros((ROUTED, 256), F32),
        }

        def project(block, source):
            wide = block[...].astype(F32)
            state["squares"] += wide * wide
            state["routed"] += wide * router_ref[source].astype(F32)
            scaled = (wide * gain_ref[source].astype(F32)).astype(BF16)
            state["acc"] += dot(scaled, weight_ref[source])

        finish_rows = gather(picked.at[n], blocks, (ys1, yr1, xs1, xr1, rs1, rr1), project)
        mean = jnp.sum(state["squares"], axis=1, keepdims=True) * (1.0 / (32 * 256))
        inverse_rms = lax.rsqrt(mean + norm_epsilon)
        product = state["acc"] * inverse_rms
        swapped = jnp.where(even, pltpu.roll(product, 255, 1), pltpu.roll(product, 1, 1))
        turned = (product * cos_ref[n] + swapped * sin_ref[n]).astype(BF16)

        tiles = dot_nt(tile_place, turned[:, 128:])
        for k in range(KV_HEADS):
            kv_tiles[k, :, 0:ROUTED] = tiles[8 * k : 8 * k + 8, :]

        def ky_copy(j, source_y):
            return remote(
                kv_tiles.at[lax.div(at_y(j), 2)], kv_all.at[x, source_y], kys.at[j], kyr.at[j], dev(at_y(j), x)
            )

        def kx_copy(j, src_x):
            return remote(kv_all.at[src_x], kv_all.at[src_x], kxs.at[j], kxr.at[j], dev(y, at_x(j)))

        for j in (4, 3, 5, 2, 6, 1, 7):
            ky_copy(j, y).start()
        kv_all[x, y] = kv_tiles[lax.div(y, 2)]
        queries = dot(turned[:, :128], key_place).astype(BF16)
        logits = jnp.sum(state["routed"], axis=1, keepdims=True)
        gate = 1.0 / (1.0 + jnp.exp(-logits))
        for j in range(1, NY):
            ky_copy(j, at_y(-j)).wait_recv()
        for j in (2, 1, 3):
            kx_copy(j, x).start()
        finish_rows()
        for j in range(1, NX):
            kx_copy(j, at_x(-j)).wait_recv()
        kv = kv_all[...].reshape(256, 128).astype(BF16)
        scores = dot(queries, kv) * (1.0 / math.sqrt(HEAD_DIM))
        scores = jnp.where(seen_ref[n] > 0.0, scores, -1e30)
        exponent = jnp.exp(scores - jnp.max(scores, axis=1, keepdims=True))
        weights = (exponent / jnp.sum(exponent, axis=1, keepdims=True)).astype(BF16)
        attended = dot_nt(weights, kv).astype(BF16)
        att[...] = dot(attended, value_place).astype(BF16)
        for j in range(1, NY):
            ky_copy(j, y).wait_send()
        for j in range(1, NX):
            kx_copy(j, x).wait_send()

        state["update"] = jnp.zeros((ROUTED, 256), F32)

        def project_out(block, source):
            state["update"] += dot(block[...], out_weight_ref[source])

        finish_att = gather(att, att_blocks, (ys3, yr3, xs3, xr3, rs3, rr3), project_out)
        new_rows = (picked[n].astype(F32) + gate * state["update"]).astype(BF16)

        @pl.when(n > 0)
        def _():
            hid_copy(n - 1).wait_recv()

        spread = dot_tn(rows_ref[n], new_rows).astype(BF16)
        covered = dot_tn(rows_ref[n], ones)
        covered = jnp.concatenate([covered, covered], axis=1)
        result = jnp.where(covered > 0.5, spread.astype(F32), hid[n].astype(F32)).astype(BF16)
        hid[n] = result

        @pl.when(n < TICKS - 1)
        def _():
            picked_out[n] = dot(next_rows_ref[n], result).astype(BF16)
            picked_copy(n).start()

        hid_copy(n).start()
        finish_att()
        return carry

    lax.fori_loop(0, TICKS, tick, 0)
    hid_copy(TICKS - 1).wait_recv()
    o_ref[...] = hid[TICKS]

    def drain(n, carry):
        hid_copy(n).wait_send()

        @pl.when(n < TICKS - 1)
        def _():
            picked_copy(n).wait_send()

        return carry

    lax.fori_loop(0, TICKS, drain, 0)


def on_device(hidden_in, positions, routed_rows, gain, router, w_query, w_key, w_value, w_out):
    sections = lax.axis_size("section")
    s = lax.axis_index("section")
    m = lax.axis_index("mp")
    tokens, width = hidden_in.shape[1:]
    peers = NX * NY
    token_rows = lax.dynamic_index_in_dim(routed_rows, s, 1, keepdims=False)
    after_rows = lax.dynamic_index_in_dim(routed_rows, (s + 1) % sections, 1, keepdims=False)
    after_rows = jnp.concatenate([after_rows[1:], after_rows[:1]], axis=0)
    token = jnp.arange(tokens, dtype=jnp.int32)
    hot = token_rows[:, :, None] == token
    rows = hot.astype(BF16)
    next_rows = (after_rows[:, :, None] == token).astype(BF16)
    doubled = jnp.concatenate([positions, positions], axis=0)
    held = lax.dynamic_slice_in_dim(doubled, s + sections - TICKS + 1, TICKS, 0)[::-1]
    row_positions = jnp.sum(jnp.where(hot, held[:, None, :], 0), axis=2)

    column = jnp.arange(256, dtype=jnp.int32)
    key_width = w_key.shape[2]
    is_query = column < HEAD_DIM
    pair = jnp.where(is_query, column // 2, (m * key_width + column - HEAD_DIM) // (2 * KV_HEADS))
    frequency = jnp.exp(pair.astype(F32) * (-2.0 * math.log(rope_base) / HEAD_DIM))
    angles = row_positions.astype(F32)[:, :, None] * frequency
    turns = column < HEAD_DIM + key_width
    cosine = jnp.where(turns, jnp.cos(angles), 1.0)
    sine = jnp.where(turns, jnp.where(column % 2 == 0, -1.0, 1.0) * jnp.sin(angles), 0.0)

    others = jnp.pad(token_rows, ((0, 0), (0, 128 - ROUTED)), constant_values=1 << 20)[:, None, :]
    distance = token_rows[:, :, None] - others
    seen = ((distance >= 0) & (distance <= row_positions[:, :, None])).astype(F32)

    spare = jnp.zeros((w_query.shape[1], 256 - HEAD_DIM - 2 * key_width), BF16)
    weight = jnp.concatenate([w_query[0], w_key[0], w_value[0], spare], axis=1).reshape(peers, 256, 256)
    vmem = pl.BlockSpec(memory_space=pltpu.VMEM)
    dma = pltpu.SemaphoreType.DMA
    sems = [dma((NY,)), dma((NY,)), dma((2 * NY,)), dma((2 * NY,)), dma((NY,)), dma((NY,))]
    out = pl.pallas_call(
        functools.partial(kernel, sections),
        out_shape=jax.ShapeDtypeStruct((tokens, width), BF16),
        in_specs=[vmem] * 10,
        out_specs=vmem,
        scratch_shapes=[
            pltpu.VMEM((TICKS + 1, tokens, width), BF16),
            pltpu.VMEM((TICKS, ROUTED, 256), BF16),
            pltpu.VMEM((TICKS, ROUTED, 256), BF16),
            pltpu.VMEM((peers, ROUTED, 256), BF16),
            pltpu.VMEM((KV_HEADS, 8, 128), F32),
            pltpu.VMEM((NX, NY, 8, 128), F32),
            pltpu.VMEM((ROUTED, HEAD_DIM), BF16),
            pltpu.VMEM((peers, ROUTED, HEAD_DIM), BF16),
            dma((TICKS,)), dma((TICKS + 1,)), dma((TICKS,)), dma((TICKS + 1,)),
            *sems, *sems,
            dma((NY,)), dma((NY,)), dma((NX,)), dma((NX,)),
        ],
        compiler_params=pltpu.CompilerParams(collective_id=0, has_side_effects=True),
    )(
        hidden_in[0],
        weight,
        w_out[0].reshape(peers, HEAD_DIM, 256),
        gain[0].reshape(peers, 1, 256),
        router[0].reshape(peers, 1, 256),
        cosine,
        sine,
        seen,
        rows,
        next_rows,
    )
    return out[None, :, :]


def solution(mesh):
    placed = (
        P("section", None, "mp"),
        P(),
        P(),
        P("section", None),
        P("section", None),
        P("section", None, "mp"),
        P("section", None, "mp"),
        P("section", None, "mp"),
        P("section", None, "mp"),
    )
    return jax.shard_map(
        on_device, mesh=mesh, in_specs=placed, out_specs=P("section", None, "mp"), check_vma=False
    )
```

time: 1430 us -> 487 us (0.34)
  blocking collectives: 1000 us -> 0 us
  Pallas kernels: 0 us -> 470 us
  starting transfers between devices: 295 us -> 0 us
  matrix products: 40.1 us -> 0 us
  local copies, waits for them, and re-layouts: 34.8 us -> 6.35 us
  waiting for transfers between devices: 26.8 us -> 0 us
    all_gather x32 -> x0, blocking collectives: 1000 us -> none  [the longest x8 291 us: on_device(): lax.all_gather(attended, 'mp', axis=1, tiled=True)]
    pallas_call x0 -> x1, Pallas kernels: none -> 470 us  [on_device(): pl.pallas_call(functools.partial(kernel, sections), out_shape=jax.ShapeDt...]
    ppermute x8 -> x0, starting transfers between devices: 295 us -> none  [from_behind(): lax.ppermute(shard, axis, [(i, (i + by) % count) for i in range(count)])]
    dot_general x56 -> x0, matrix products: 40.1 us -> none  [the longest x8 22.1 us: on_device(): jnp.dot(normed, query_weight, preferred_element_type=jnp.float32)]
    ppermute x8 -> x0, waiting for transfers between devices: 26.8 us -> none  [from_behind(): lax.ppermute(shard, axis, [(i, (i + by) % count) for i in range(count)])]
  transfers between devices with their start and end apart: 8 -> 0, of which waited for: 7 -> 0; matrix products, arithmetic and copies ran while one was open for 1% -> 0% of each run, Pallas kernels for 0% -> 0%
where the time goes in v1:
time: 487 us
  Pallas kernels  470 us (97%)
  other arithmetic  10.1 us (2%)
  local copies, waits for them, and re-layouts  6.35 us (1%)
    pallas_call x1, Pallas kernels, on_device(): pl.pallas_call(functools.partial(kernel, sections), out_shape=jax.ShapeDt...  470 us

profile of v1, /device:TPU:1, one launch (start us, length us, event | category | flops | bytes accessed | tf_op | source)
XLA Modules:
  0.0 486.8 jit_solution(4406117762411021655)
XLA Ops:
  0.0 0.0 copy-start
  0.0 1.9 copy.13
  1.9 2.6 copy.12
  4.5 0.1 pad.12.clone
  4.6 0.0 copy-start.1
  4.6 5.3 %maximum_maximum_fusion.weight_ref = bf16[32,256,256]{2,1,0:T(8,128)(2,1)} fusion(bf16[32,256,16]{2,1,0:T(8,128)(2,1)S(1)} %bitcast.17, bf16[32,256,16]{2,1,0:T(8,128)(2,1)} %bitcast.18, bf16[32,256,128]{2,1,0:T(8,128)(2,1)} %bitcast.19, bf16[256]{0:T(256)(128)(2,1)S(1)} %pad.12.clone), kind=kLoop, calls=%fused_computation | loop fusion | flops 16777216 | bytes 6816256 | tf_op jit(solution)/shard_map/concatenate | solution.py:306
  9.9 0.0 copy-done.1
  10.0 0.1 rev.3
  10.0 0.0 copy-done
  10.1 0.3 select_reduce_fusion
  10.4 2.6 fusion.4
  13.0 0.8 fusion.6.seen_ref
  13.9 1.0 fusion
  14.9 470.3 %shard_map.91 = bf16[384,256]{1,0:T(8,128)(2,1)} custom-call(bf16[384,256]{1,0:T(8,128)(2,1)} %bitcast.22, bf16[32,256,256]{2,1,0:T(8,128)(2,1)} %maximum_maximum_fusion.weight_ref, bf16[32,128,256]{2,1,0:T(8,128)(2,1)} %bitcast.20, bf16[32,1,256]{2,1,0:T(2,128)(2,1)} %bitcast.27, bf16[32,1,256]{2,1,0:T(2,128)(2,1)} %bitcast.28, ...), custom_call_target="tpu_custom_call" | custom-call | tf_op jit(solution)/shard_map/pallas_call | solution.py:310
  485.2 1.6 copy.21
  (11 shorter events, 0.1 us)
Async XLA Ops:
  0.0 10.0 %copy-start = (s32[8,16,48]{2,1,0:T(8,128)S(1)}, s32[8,16,48]{2,1,0:T(8,128)}, u32[]{:S(2)}) copy-start(s32[8,16,48]{2,1,0:T(8,128)} %param.11) | copy-start | bytes 73732
  4.6 5.3 %copy-start.1 = (s32[16,384]{1,0:T(8,128)S(1)}, s32[16,384]{1,0:T(8,128)}, u32[]{:S(2)}) copy-start(s32[16,384]{1,0:T(8,128)} %param.10) | copy-start | bytes 73732

commit v2 on v1

--- a/solution.py
+++ b/solution.py
@@ -22,6 +22,7 @@
 MESH = pl.DeviceIdType.MESH
 F32 = jnp.float32
 BF16 = jnp.bfloat16
+CHUNKS = ((0, 4), (4, 8))
 ORDER = (0, 1, 7, 2, 6, 3, 5, 4)
 
 
@@ -79,55 +80,56 @@
         ys, yr, xs, xr, rs, rr = sems
         right = dev(y, at_x(1))
         left = dev(y, at_x(-1))
-
-        def slot(j, xx):
-            return at_y(-j) * NX + xx
-
-        def y_copy(j, source_y):
-            return remote(own, into.at[source_y * NX + x], ys.at[j], yr.at[j], dev(at_y(j), x))
-
-        def x_copy(j, way, src, src_x):
+        chunks = CHUNKS
+
+        def y_copy(t, dest_x):
+            return remote(own, into.at[x, t], ys.at[t], yr.at[t], dev(at_y(ORDER[t]), dest_x))
+
+        def part(c, xx):
+            first, last = chunks[c]
+            return into.at[xx, pl.ds(first, last - first)]
+
+        def x_copy(c, way, xx):
             to = right if way == 0 else left
-            return remote(src, into.at[slot(j, src_x)], xs.at[2 * j + way], xr.at[2 * j + way], to)
-
-        def r_copy(j, src_x):
-            to = right if j % 2 == 0 else left
-            block = into.at[slot(j, src_x)]
-            return remote(block, block, rs.at[j], rr.at[j], to)
-
-        for j in (4, 3, 5, 2, 6, 1, 7):
-            y_copy(j, y).start()
+            return remote(part(c, xx), part(c, xx), xs.at[2 * c + way], xr.at[2 * c + way], to)
+
+        def r_copy(c, xx):
+            to = right if c % 2 == 0 else left
+            return remote(part(c, xx), part(c, xx), rs.at[c], rr.at[c], to)
+
+        def use(c, xx):
+            for t in range(*chunks[c]):
+                consume(into.at[xx, t], at_y(-ORDER[t]) * NX + xx)
+
+        for t in range(1, NY):
+            y_copy(t, x).start()
+        into[x, 0] = own[...]
         sent = []
-        for t in range(NY + 2):
-            if t < NY:
-                j = ORDER[t]
-                if j == 0:
-                    mine = own
-                else:
-                    y_copy(j, at_y(-j)).wait_recv()
-                    mine = into.at[slot(j, x)]
+        for c in range(len(chunks) + 2):
+            if c < len(chunks):
+                for t in range(max(chunks[c][0], 1), chunks[c][1]):
+                    y_copy(t, x).wait_recv()
                 for way in (0, 1):
-                    copy = x_copy(j, way, mine, x)
+                    copy = x_copy(c, way, x)
                     copy.start()
                     sent.append(copy)
-                consume(mine, slot(j, x))
-            if 1 <= t <= NY:
-                j = ORDER[t - 1]
-                for way, src_x in ((0, at_x(-1)), (1, at_x(1))):
-                    x_copy(j, way, into.at[slot(j, src_x)], src_x).wait_recv()
-                    if j % 2 == way:
-                        copy = r_copy(j, src_x)
+                use(c, x)
+            if 1 <= c <= len(chunks):
+                for way, xx in ((0, at_x(-1)), (1, at_x(1))):
+                    x_copy(c - 1, way, xx).wait_recv()
+                    if (c - 1) % 2 == way:
+                        copy = r_copy(c - 1, xx)
                         copy.start()
                         sent.append(copy)
-                    consume(into.at[slot(j, src_x)], slot(j, src_x))
-            if t >= 2:
-                j = ORDER[t - 2]
-                r_copy(j, at_x(2)).wait_recv()
-                consume(into.at[slot(j, at_x(2))], slot(j, at_x(2)))
+                for xx in (at_x(-1), at_x(1)):
+                    use(c - 1, xx)
+            if c >= 2:
+                r_copy(c - 2, at_x(2)).wait_recv()
+                use(c - 2, at_x(2))
 
         def finish():
-            for j in range(1, NY):
-                y_copy(j, y).wait_send()
+            for t in range(1, NY):
+                y_copy(t, x).wait_send()
             for copy in sent:
                 copy.wait_send()
 
@@ -316,11 +318,11 @@
             pltpu.VMEM((TICKS + 1, tokens, width), BF16),
             pltpu.VMEM((TICKS, ROUTED, 256), BF16),
             pltpu.VMEM((TICKS, ROUTED, 256), BF16),
-            pltpu.VMEM((peers, ROUTED, 256), BF16),
+            pltpu.VMEM((NX, NY, ROUTED, 256), BF16),
             pltpu.VMEM((KV_HEADS, 8, 128), F32),
             pltpu.VMEM((NX, NY, 8, 128), F32),
             pltpu.VMEM((ROUTED, HEAD_DIM), BF16),
-            pltpu.VMEM((peers, ROUTED, HEAD_DIM), BF16),
+            pltpu.VMEM((NX, NY, ROUTED, HEAD_DIM), BF16),
             dma((TICKS,)), dma((TICKS + 1,)), dma((TICKS,)), dma((TICKS + 1,)),
             *sems, *sems,
             dma((NY,)), dma((NY,)), dma((NX,)), dma((NX,)),

time: 487 us -> 353 us (0.72)
  Pallas kernels: 470 us -> 336 us
    pallas_call x1, Pallas kernels: 470 us -> 336 us  [on_device(): pl.pallas_call(functools.partial(kernel, sections), out_shape=jax.ShapeDt...]
where the time goes in v2:
time: 353 us
  Pallas kernels  336 us (95%)
  other arithmetic  10.1 us (3%)
  local copies, waits for them, and re-layouts  6.35 us (2%)
    pallas_call x1, Pallas kernels, on_device(): pl.pallas_call(functools.partial(kernel, sections), out_shape=jax.ShapeDt...  336 us

profile of v2, /device:TPU:1, one launch (start us, length us, event | category | flops | bytes accessed | tf_op | source)
XLA Modules:
  0.0 352.9 jit_solution(13475572963194984931)
XLA Ops:
  0.0 0.0 copy-start
  0.0 1.9 copy.13
  1.9 2.6 copy.12
  4.5 0.1 pad.12.clone
  4.6 0.0 copy-start.1
  4.6 5.3 %maximum_maximum_fusion.weight_ref = bf16[32,256,256]{2,1,0:T(8,128)(2,1)} fusion(bf16[32,256,16]{2,1,0:T(8,128)(2,1)S(1)} %bitcast.17, bf16[32,256,16]{2,1,0:T(8,128)(2,1)} %bitcast.18, bf16[32,256,128]{2,1,0:T(8,128)(2,1)} %bitcast.19, bf16[256]{0:T(256)(128)(2,1)S(1)} %pad.12.clone), kind=kLoop, calls=%fused_computation | loop fusion | flops 16777216 | bytes 6816256 | tf_op jit(solution)/shard_map/concatenate | solution.py:308
  9.9 0.0 copy-done.1
  10.0 0.1 rev.3
  10.0 0.0 copy-done
  10.1 0.3 select_reduce_fusion
  10.4 2.6 fusion.4
  13.0 0.8 fusion.6.seen_ref
  13.9 1.0 fusion
  14.9 336.4 %shard_map.91 = bf16[384,256]{1,0:T(8,128)(2,1)} custom-call(bf16[384,256]{1,0:T(8,128)(2,1)} %bitcast.22, bf16[32,256,256]{2,1,0:T(8,128)(2,1)} %maximum_maximum_fusion.weight_ref, bf16[32,128,256]{2,1,0:T(8,128)(2,1)} %bitcast.20, bf16[32,1,256]{2,1,0:T(2,128)(2,1)} %bitcast.27, bf16[32,1,256]{2,1,0:T(2,128)(2,1)} %bitcast.28, ...), custom_call_target="tpu_custom_call" | custom-call | tf_op jit(solution)/shard_map/pallas_call | solution.py:312
  351.3 1.6 copy.21
  (11 shorter events, 0.1 us)
Async XLA Ops:
  0.0 10.0 %copy-start = (s32[8,16,48]{2,1,0:T(8,128)S(1)}, s32[8,16,48]{2,1,0:T(8,128)}, u32[]{:S(2)}) copy-start(s32[8,16,48]{2,1,0:T(8,128)} %param.11) | copy-start | bytes 73732
  4.6 5.3 %copy-start.1 = (s32[16,384]{1,0:T(8,128)S(1)}, s32[16,384]{1,0:T(8,128)}, u32[]{:S(2)}) copy-start(s32[16,384]{1,0:T(8,128)} %param.10) | copy-start | bytes 73732

commit v3 on v2

--- a/solution.py
+++ b/solution.py
@@ -22,7 +22,6 @@
 MESH = pl.DeviceIdType.MESH
 F32 = jnp.float32
 BF16 = jnp.bfloat16
-CHUNKS = ((0, 4), (4, 8))
 ORDER = (0, 1, 7, 2, 6, 3, 5, 4)
 
 
@@ -76,11 +75,10 @@
             src_ref=src, dst_ref=dst, send_sem=send, recv_sem=recv, device_id=to, device_id_type=MESH
         )
 
-    def gather(own, into, sems, consume):
+    def gather(own, into, sems, consume, chunks, direct):
         ys, yr, xs, xr, rs, rr = sems
         right = dev(y, at_x(1))
         left = dev(y, at_x(-1))
-        chunks = CHUNKS
 
         def y_copy(t, dest_x):
             return remote(own, into.at[x, t], ys.at[t], yr.at[t], dev(at_y(ORDER[t]), dest_x))
@@ -95,6 +93,8 @@
 
         def r_copy(c, xx):
             to = right if c % 2 == 0 else left
+            if direct:
+                to = dev(y, at_x(2))
             return remote(part(c, xx), part(c, xx), rs.at[c], rr.at[c], to)
 
         def use(c, xx):
@@ -109,6 +109,10 @@
             if c < len(chunks):
                 for t in range(max(chunks[c][0], 1), chunks[c][1]):
                     y_copy(t, x).wait_recv()
+                if direct:
+                    copy = r_copy(c, x)
+                    copy.start()
+                    sent.append(copy)
                 for way in (0, 1):
                     copy = x_copy(c, way, x)
                     copy.start()
@@ -117,7 +121,7 @@
             if 1 <= c <= len(chunks):
                 for way, xx in ((0, at_x(-1)), (1, at_x(1))):
                     x_copy(c - 1, way, xx).wait_recv()
-                    if (c - 1) % 2 == way:
+                    if not direct and (c - 1) % 2 == way:
                         copy = r_copy(c - 1, xx)
                         copy.start()
                         sent.append(copy)
@@ -186,7 +190,7 @@
             scaled = (wide * gain_ref[source].astype(F32)).astype(BF16)
             state["acc"] += dot(scaled, weight_ref[source])
 
-        finish_rows = gather(picked.at[n], blocks, (ys1, yr1, xs1, xr1, rs1, rr1), project)
+        finish_rows = gather(picked.at[n], blocks, (ys1, yr1, xs1, xr1, rs1, rr1), project, ((0, 4), (4, 8)), True)
         mean = jnp.sum(state["squares"], axis=1, keepdims=True) * (1.0 / (32 * 256))
         inverse_rms = lax.rsqrt(mean + norm_epsilon)
         product = state["acc"] * inverse_rms
@@ -235,7 +239,7 @@
         def project_out(block, source):
             state["update"] += dot(block[...], out_weight_ref[source])
 
-        finish_att = gather(att, att_blocks, (ys3, yr3, xs3, xr3, rs3, rr3), project_out)
+        finish_att = gather(att, att_blocks, (ys3, yr3, xs3, xr3, rs3, rr3), project_out, ((0, 4), (4, 8)), True)
         new_rows = (picked[n].astype(F32) + gate * state["update"]).astype(BF16)
 
         @pl.when(n > 0)

time: 353 us -> 327 us (0.926)
  Pallas kernels: 336 us -> 308 us
    pallas_call x1, Pallas kernels: 336 us -> 308 us  [on_device(): pl.pallas_call(functools.partial(kernel, sections), out_shape=jax.ShapeDt...]
where the time goes in v3:
time: 327 us; the launch traced here: 325 us
  Pallas kernels  308 us (94%)
  other arithmetic  10.1 us (3%)
  local copies, waits for them, and re-layouts  6.35 us (2%)
    pallas_call x1, Pallas kernels, on_device(): pl.pallas_call(functools.partial(kernel, sections), out_shape=jax.ShapeDt...  308 us

profile of v3, /device:TPU:1, one launch (start us, length us, event | category | flops | bytes accessed | tf_op | source)
XLA Modules:
  0.0 324.8 jit_solution(7847314560020723308)
XLA Ops:
  0.0 0.0 copy-start
  0.0 1.9 copy.13
  1.9 2.6 copy.12
  4.5 0.1 pad.12.clone
  4.6 0.0 copy-start.1
  4.6 5.3 %maximum_maximum_fusion.weight_ref = bf16[32,256,256]{2,1,0:T(8,128)(2,1)} fusion(bf16[32,256,16]{2,1,0:T(8,128)(2,1)S(1)} %bitcast.17, bf16[32,256,16]{2,1,0:T(8,128)(2,1)} %bitcast.18, bf16[32,256,128]{2,1,0:T(8,128)(2,1)} %bitcast.19, bf16[256]{0:T(256)(128)(2,1)S(1)} %pad.12.clone), kind=kLoop, calls=%fused_computation | loop fusion | flops 16777216 | bytes 6816256 | tf_op jit(solution)/shard_map/concatenate | solution.py:312
  9.9 0.0 copy-done.1
  10.0 0.1 rev.3
  10.0 0.0 copy-done
  10.1 0.3 select_reduce_fusion
  10.4 2.6 fusion.4
  13.0 0.8 fusion.6.seen_ref
  13.9 1.0 fusion
  14.9 308.3 %shard_map.91 = bf16[384,256]{1,0:T(8,128)(2,1)} custom-call(bf16[384,256]{1,0:T(8,128)(2,1)} %bitcast.22, bf16[32,256,256]{2,1,0:T(8,128)(2,1)} %maximum_maximum_fusion.weight_ref, bf16[32,128,256]{2,1,0:T(8,128)(2,1)} %bitcast.20, bf16[32,1,256]{2,1,0:T(2,128)(2,1)} %bitcast.27, bf16[32,1,256]{2,1,0:T(2,128)(2,1)} %bitcast.28, ...), custom_call_target="tpu_custom_call" | custom-call | tf_op jit(solution)/shard_map/pallas_call | solution.py:316
  323.2 1.6 copy.21
  (11 shorter events, 0.1 us)
Async XLA Ops:
  0.0 10.0 %copy-start = (s32[8,16,48]{2,1,0:T(8,128)S(1)}, s32[8,16,48]{2,1,0:T(8,128)}, u32[]{:S(2)}) copy-start(s32[8,16,48]{2,1,0:T(8,128)} %param.11) | copy-start | bytes 73732
  4.6 5.3 %copy-start.1 = (s32[16,384]{1,0:T(8,128)S(1)}, s32[16,384]{1,0:T(8,128)}, u32[]{:S(2)}) copy-start(s32[16,384]{1,0:T(8,128)} %param.10) | copy-start | bytes 73732
